TPU v7x, 32 devices: a whole 2x2x4 slice. The times are simulated.
32 devices in a mesh: shard: 2 (over y), context: 4 (over z), tensor: 4 (over x, core).
Axes of the slice: x: 2, y: 2, z: 4, core: 2. Of those that a mesh axis runs over, the one named last changes fastest.
Arguments:
- inputs: bfloat16 [6, 2048, 768], P('shard', 'context'), may hold values from -6 to 6
- w_query: bfloat16 [768, 768], P('shard', 'tensor'), may hold values from -0.21875 to 0.21875
- b_query: float32 [768], P('tensor'), may hold values from -3 to 3
- w_key: bfloat16 [768, 768], P('shard', 'tensor'), may hold values from -0.21875 to 0.21875
- w_value: bfloat16 [768, 768], P('shard', 'tensor'), may hold values from -0.21875 to 0.21875
- b_value: float32 [768], P('tensor'), may hold values from -3 to 3
- w_out: bfloat16 [768, 768], P('tensor', 'shard'), may hold values from -3.5 to 3.5
- b_out: float32 [768], replicated, may hold values from -3 to 3
- first_gain: float32 [768], replicated, may hold values from 0.5 to 1.5
- first_bias: float32 [768], replicated, may hold values from -2 to 2
- w_hidden: bfloat16 [768, 3072], P('shard', 'tensor'), may hold values from -0.21875 to 0.21875
- b_hidden: float32 [3072], P('tensor'), may hold values from -3 to 3
- w_down: bfloat16 [3072, 768], P('tensor', 'shard'), may hold values from -0.109375 to 0.109375
- b_down: float32 [768], replicated, may hold values from -3 to 3
- second_gain: float32 [768], replicated, may hold values from 0.5 to 1.5
- second_bias: float32 [768], replicated, may hold values from -2 to 2
- cotangent: bfloat16 [6, 2048, 768], P('shard', 'context'), may hold values from -6 to 6
Outputs:
- outputs: bfloat16 [6, 2048, 768], P('shard', 'context')
- input_grad: bfloat16 [6, 2048, 768], P('shard', 'context')
- grad_w_query: float32 [768, 768], P('shard', 'tensor')
- grad_b_query: float32 [768], P('tensor')
- grad_w_key: float32 [768, 768], P('shard', 'tensor')
- grad_w_value: float32 [768, 768], P('shard', 'tensor')
- grad_b_value: float32 [768], P('tensor')
- grad_w_out: float32 [768, 768], P('tensor', 'shard')
- grad_b_out: float32 [768], replicated
- grad_first_gain: float32 [768], replicated
- grad_first_bias: float32 [768], replicated
- grad_w_hidden: float32 [768, 3072], P('shard', 'tensor')
- grad_b_hidden: float32 [3072], P('tensor')
- grad_w_down: float32 [3072, 768], P('tensor', 'shard')
- grad_b_down: float32 [768], replicated
- grad_second_gain: float32 [768], replicated
- grad_second_bias: float32 [768], replicated
All inputs are finite; a program needn't handle non-finite values.
Results may differ from a plain program's by a relative error of at most 0.018.
Values may be sent and summed in bfloat16 or wider, within the bound.
No kernel may reach another device: no remote copies, remote signals or barrier semaphores. Data moves between devices by JAX's collectives and lax.ppermute only.
A program may use at most 256 MiB of HBM per device.

v0:
```python
import jax
import jax.numpy as jnp
from jax import lax
from jax.sharding import PartitionSpec as P

HEAD_DIM = 64
MICRO = 3
EPSILON = 1e-05


def layer_norm(values, gain, bias):
    centre = jnp.mean(values, axis=-1, keepdims=True)
    centred = values - centre
    inverse = lax.rsqrt(jnp.mean(centred * centred, axis=-1, keepdims=True) + EPSILON)
    normed = centred * inverse
    return (normed * gain + bias, normed, inverse)


def norm_back(grad, normed, inverse, gain):
    scaled = grad * gain
    return inverse * (
        scaled
        - jnp.mean(scaled, axis=-1, keepdims=True)
        - normed * jnp.mean(scaled * normed, axis=-1, keepdims=True)
    )


def gelu_exact(values):
    return jax.nn.gelu(values, approximate=False)


def attend(queries, keys, values, factor):
    heads_here = queries.shape[-1] // HEAD_DIM
    results = []
    totals = []
    for head in range(heads_here):
        lower = head * HEAD_DIM
        upper = lower + HEAD_DIM
        scores = (
            jnp.einsum(
                "sqd,skd->sqk",
                queries[..., lower:upper],
                keys[..., lower:upper],
                preferred_element_type=jnp.float32,
            )
            * factor
        )
        log_total = jax.nn.logsumexp(scores, axis=-1, keepdims=True)
        low_probs = jnp.exp(scores - log_total).astype(jnp.bfloat16)
        results.append(
            jnp.einsum(
                "sqk,skd->sqd",
                low_probs,
                values[..., lower:upper],
                preferred_element_type=jnp.float32,
            )
        )
        totals.append(log_total)
    return (jnp.concatenate(results, axis=-1).astype(jnp.bfloat16), totals)


def attend_back(queries, keys, values, grad_heads, totals, factor):
    heads_here = queries.shape[-1] // HEAD_DIM
    grad_queries = []
    grad_keys = []
    grad_values = []
    for head in range(heads_here):
        lower = head * HEAD_DIM
        upper = lower + HEAD_DIM
        query_head = queries[..., lower:upper]
        key_head = keys[..., lower:upper]
        grad_head = grad_heads[..., lower:upper]
        scores = (
            jnp.einsum("sqd,skd->sqk", query_head, key_head, preferred_element_type=jnp.float32)
            * factor
        )
        attn_probs = jnp.exp(scores - totals[head])
        low_probs = attn_probs.astype(jnp.bfloat16)
        grad_probs = jnp.einsum(
            "sqd,skd->sqk", grad_head, values[..., lower:upper], preferred_element_type=jnp.float32
        )
        grad_values.append(
            jnp.einsum("sqk,sqd->skd", low_probs, grad_head, preferred_element_type=jnp.float32)
        )
        weighted = jnp.sum(attn_probs * grad_probs, axis=-1, keepdims=True)
        grad_scores = (attn_probs * (grad_probs - weighted)).astype(jnp.bfloat16)
        grad_queries.append(
            jnp.einsum("sqk,skd->sqd", grad_scores, key_head, preferred_element_type=jnp.float32)
            * factor
        )
        grad_keys.append(
            jnp.einsum("sqk,sqd->skd", grad_scores, query_head, preferred_element_type=jnp.float32)
            * factor
        )
    return (
        jnp.concatenate(grad_queries, axis=-1),
        jnp.concatenate(grad_keys, axis=-1),
        jnp.concatenate(grad_values, axis=-1),
    )


def on_device(
    inputs,
    w_query,
    b_query,
    w_key,
    w_value,
    b_value,
    w_out,
    b_out,
    first_gain,
    first_bias,
    w_hidden,
    b_hidden,
    w_down,
    b_down,
    second_gain,
    second_bias,
    cotangent,
):
    seq_count, part_len, width = inputs.shape
    per_micro = seq_count // MICRO
    row_count = per_micro * part_len
    head_cols = w_query.shape[1]
    hidden_cols = w_hidden.shape[1]
    factor = HEAD_DIM ** (-0.5)
    acc_query = jnp.zeros((width, head_cols), jnp.float32)
    acc_key = jnp.zeros((width, head_cols), jnp.float32)
    acc_value = jnp.zeros((width, head_cols), jnp.float32)
    acc_out = jnp.zeros((head_cols, width), jnp.float32)
    acc_hidden = jnp.zeros((width, hidden_cols), jnp.float32)
    acc_down = jnp.zeros((hidden_cols, width), jnp.float32)
    sum_b_query = jnp.zeros((head_cols,), jnp.float32)
    sum_b_value = jnp.zeros((head_cols,), jnp.float32)
    sum_b_out = jnp.zeros((width,), jnp.float32)
    sum_first_gain = jnp.zeros((width,), jnp.float32)
    sum_first_bias = jnp.zeros((width,), jnp.float32)
    sum_b_hidden = jnp.zeros((hidden_cols,), jnp.float32)
    sum_b_down = jnp.zeros((width,), jnp.float32)
    sum_second_gain = jnp.zeros((width,), jnp.float32)
    sum_second_bias = jnp.zeros((width,), jnp.float32)
    result_parts = []
    input_parts = []
    for batch_index in range(MICRO):
        full = (
            lax.all_gather(w_query, "shard", axis=0, tiled=True),
            lax.all_gather(w_key, "shard", axis=0, tiled=True),
            lax.all_gather(w_value, "shard", axis=0, tiled=True),
            lax.all_gather(w_out, "shard", axis=1, tiled=True),
            lax.all_gather(w_hidden, "shard", axis=0, tiled=True),
            lax.all_gather(w_down, "shard", axis=1, tiled=True),
        )
        full_query, full_key, full_value, full_out, full_hidden, full_down = full
        begin = batch_index * per_micro
        token_rows = inputs[begin : begin + per_micro].reshape(row_count, width)
        query_low = (
            jnp.dot(token_rows, full_query, preferred_element_type=jnp.float32) + b_query
        ).astype(jnp.bfloat16)
        key_low = jnp.dot(token_rows, full_key, preferred_element_type=jnp.float32).astype(
            jnp.bfloat16
        )
        value_low = (
            jnp.dot(token_rows, full_value, preferred_element_type=jnp.float32) + b_value
        ).astype(jnp.bfloat16)
        queries = query_low.reshape(per_micro, part_len, head_cols)
        local_keys = key_low.reshape(per_micro, part_len, head_cols)
        local_values = value_low.reshape(per_micro, part_len, head_cols)
        all_keys, all_values = (
            lax.all_gather(local_keys, "context", axis=1, tiled=True),
            lax.all_gather(local_values, "context", axis=1, tiled=True),
        )
        attended, totals = attend(queries, all_keys, all_values, factor)
        attended_rows = attended.reshape(row_count, head_cols)
        branch = lax.psum(
            jnp.dot(attended_rows, full_out, preferred_element_type=jnp.float32), "tensor"
        )
        first, normed_first, inverse_first = layer_norm(
            token_rows.astype(jnp.float32) + branch + b_out, first_gain, first_bias
        )
        first_low = first.astype(jnp.bfloat16)
        inner = jnp.dot(first_low, full_hidden, preferred_element_type=jnp.float32) + b_hidden
        activated, gelu_back = jax.vjp(gelu_exact, inner)
        activated_low = activated.astype(jnp.bfloat16)
        ffn = lax.psum(
            jnp.dot(activated_low, full_down, preferred_element_type=jnp.float32), "tensor"
        )
        result, normed_second, inverse_second = layer_norm(
            first + ffn + b_down, second_gain, second_bias
        )
        result_parts.append(result.astype(jnp.bfloat16).reshape(per_micro, part_len, width))
        grad_result = (
            cotangent[begin : begin + per_micro].reshape(row_count, width).astype(jnp.float32)
        )
        sum_second_gain = sum_second_gain + jnp.sum(grad_result * normed_second, axis=0)
        sum_second_bias = sum_second_bias + jnp.sum(grad_result, axis=0)
        grad_second = norm_back(grad_result, normed_second, inverse_second, second_gain)
        sum_b_down = sum_b_down + jnp.sum(grad_second, axis=0)
        grad_ffn = grad_second.astype(jnp.bfloat16)
        acc_down = acc_down + jnp.einsum(
            "rf,rd->fd", activated_low, grad_ffn, preferred_element_type=jnp.float32
        )
        grad_act = jnp.einsum("rd,fd->rf", grad_ffn, full_down, preferred_element_type=jnp.float32)
        grad_inner = gelu_back(grad_act)[0].astype(jnp.bfloat16)
        sum_b_hidden = sum_b_hidden + jnp.sum(grad_inner.astype(jnp.float32), axis=0)
        acc_hidden = acc_hidden + jnp.einsum(
            "rd,rf->df", first_low, grad_inner, preferred_element_type=jnp.float32
        )
        grad_first = grad_second + lax.psum(
            jnp.einsum("rf,df->rd", grad_inner, full_hidden, preferred_element_type=jnp.float32),
            "tensor",
        )
        sum_first_gain = sum_first_gain + jnp.sum(grad_first * normed_first, axis=0)
        sum_first_bias = sum_first_bias + jnp.sum(grad_first, axis=0)
        grad_pre_first = norm_back(grad_first, normed_first, inverse_first, first_gain)
        sum_b_out = sum_b_out + jnp.sum(grad_pre_first, axis=0)
        grad_attn = grad_pre_first.astype(jnp.bfloat16)
        acc_out = acc_out + jnp.einsum(
            "rh,rd->hd", attended_rows, grad_attn, preferred_element_type=jnp.float32
        )
        grad_heads = jnp.einsum(
            "rd,hd->rh", grad_attn, full_out, preferred_element_type=jnp.float32
        ).astype(jnp.bfloat16)
        grad_heads = grad_heads.reshape(per_micro, part_len, head_cols)
        grad_queries, grad_keys, grad_values = attend_back(
            queries, all_keys, all_values, grad_heads, totals, factor
        )
        own_keys, own_values = (
            lax.psum_scatter(grad_keys, "context", scatter_dimension=1, tiled=True),
            lax.psum_scatter(grad_values, "context", scatter_dimension=1, tiled=True),
        )
        grad_query_low = grad_queries.astype(jnp.bfloat16).reshape(row_count, head_cols)
        grad_key_low = own_keys.astype(jnp.bfloat16).reshape(row_count, head_cols)
        grad_value_low = own_values.astype(jnp.bfloat16).reshape(row_count, head_cols)
        sum_b_query = sum_b_query + jnp.sum(grad_query_low.astype(jnp.float32), axis=0)
        sum_b_value = sum_b_value + jnp.sum(grad_value_low.astype(jnp.float32), axis=0)
        acc_query = acc_query + jnp.einsum(
            "rd,rh->dh", token_rows, grad_query_low, preferred_element_type=jnp.float32
        )
        acc_key = acc_key + jnp.einsum(
            "rd,rh->dh", token_rows, grad_key_low, preferred_element_type=jnp.float32
        )
        acc_value = acc_value + jnp.einsum(
            "rd,rh->dh", token_rows, grad_value_low, preferred_element_type=jnp.float32
        )
        back_rows = (
            jnp.einsum("rh,dh->rd", grad_query_low, full_query, preferred_element_type=jnp.float32)
            + jnp.einsum("rh,dh->rd", grad_key_low, full_key, preferred_element_type=jnp.float32)
            + jnp.einsum(
                "rh,dh->rd", grad_value_low, full_value, preferred_element_type=jnp.float32
            )
        )
        grad_input = grad_pre_first + lax.psum(back_rows, "tensor")
        input_parts.append(grad_input.astype(jnp.bfloat16).reshape(per_micro, part_len, width))
    matrices = (acc_query, acc_key, acc_value, acc_out, acc_hidden, acc_down)
    owned = (
        lax.psum_scatter(
            matrices[0].astype(jnp.bfloat16), "shard", scatter_dimension=0, tiled=True
        ).astype(jnp.float32),
        lax.psum_scatter(
            matrices[1].astype(jnp.bfloat16), "shard", scatter_dimension=0, tiled=True
        ).astype(jnp.float32),
        lax.psum_scatter(
            matrices[2].astype(jnp.bfloat16), "shard", scatter_dimension=0, tiled=True
        ).astype(jnp.float32),
        lax.psum_scatter(
            matrices[3].astype(jnp.bfloat16), "shard", scatter_dimension=1, tiled=True
        ).astype(jnp.float32),
        lax.psum_scatter(
            matrices[4].astype(jnp.bfloat16), "shard", scatter_dimension=0, tiled=True
        ).astype(jnp.float32),
        lax.psum_scatter(
            matrices[5].astype(jnp.bfloat16), "shard", scatter_dimension=1, tiled=True
        ).astype(jnp.float32),
    )
    owned = (
        lax.psum(owned[0].astype(jnp.bfloat16), "context").astype(jnp.float32),
        lax.psum(owned[1].astype(jnp.bfloat16), "context").astype(jnp.float32),
        lax.psum(owned[2].astype(jnp.bfloat16), "context").astype(jnp.float32),
        lax.psum(owned[3].astype(jnp.bfloat16), "context").astype(jnp.float32),
        lax.psum(owned[4].astype(jnp.bfloat16), "context").astype(jnp.float32),
        lax.psum(owned[5].astype(jnp.bfloat16), "context").astype(jnp.float32),
    )
    vectors = lax.psum(
        (
            sum_b_query,
            sum_b_value,
            sum_b_out,
            sum_first_gain,
            sum_first_bias,
            sum_b_hidden,
            sum_b_down,
            sum_second_gain,
            sum_second_bias,
        ),
        ("shard", "context"),
    )
    return (
        jnp.concatenate(result_parts, axis=0),
        jnp.concatenate(input_parts, axis=0),
        owned[0],
        vectors[0],
        owned[1],
        owned[2],
        vectors[1],
        owned[3],
        vectors[2],
        vectors[3],
        vectors[4],
        owned[4],
        vectors[5],
        owned[5],
        vectors[6],
        vectors[7],
        vectors[8],
    )


def solution(mesh):
    return jax.shard_map(
        on_device,
        mesh=mesh,
        in_specs=(
            P("shard", "context", None),
            P("shard", "tensor"),
            P("tensor"),
            P("shard", "tensor"),
            P("shard", "tensor"),
            P("tensor"),
            P("tensor", "shard"),
            P(),
            P(),
            P(),
            P("shard", "tensor"),
            P("tensor"),
            P("tensor", "shard"),
            P(),
            P(),
            P(),
            P("shard", "context", None),
        ),
        out_specs=(
            P("shard", "context", None),
            P("shard", "context", None),
            P("shard", "tensor"),
            P("tensor"),
            P("shard", "tensor"),
            P("shard", "tensor"),
            P("tensor"),
            P("tensor", "shard"),
            P(),
            P(),
            P(),
            P("shard", "tensor"),
            P("tensor"),
            P("tensor", "shard"),
            P(),
            P(),
            P(),
        ),
        check_vma=False,
    )
```

profile of v0, /device:TPU:0, one launch (start us, length us, event | category | flops | bytes accessed | tf_op | source)
XLA Modules:
  0.0 1056.1 jit_solution(5960588439616806110)
XLA Ops:
  8.1 7.7 all_gather.48
  19.7 5.8 all_gather.49
  26.8 5.8 all_gather.51
  33.9 18.1 %all-gather.4 = bf16[2048,192]{0,1:T(8,128)(2,1)S(1)} all-gather(bf16[512,192]{0,1:T(8,128)(2,1)S(1)} %convolution_convert_fusion.3), channel_id=6, replica_groups=mesh['shard'=2,'context'=4,'tensor'=4] {'context'}, dimensions={0}, use_global_device_ids=true | all-gather | bytes 983040 | tf_op jit(solution)/shard_map/all_gather | solution.py:169
  54.5 17.6 %all-gather.2 = bf16[2048,192]{0,1:T(8,128)(2,1)S(1)} all-gather(bf16[512,192]{0,1:T(8,128)(2,1)S(1)} %convolution_convert_fusion.4), channel_id=4, replica_groups=mesh['shard'=2,'context'=4,'tensor'=4] {'context'}, dimensions={0}, use_global_device_ids=true | all-gather | bytes 983040 | tf_op jit(solution)/shard_map/all_gather | solution.py:169
  74.5 15.7 %all-gather = bf16[2048,192]{0,1:T(8,128)(2,1)S(1)} all-gather(bf16[512,192]{0,1:T(8,128)(2,1)S(1)} %convolution_convert_fusion.5), channel_id=2, replica_groups=mesh['shard'=2,'context'=4,'tensor'=4] {'context'}, dimensions={0}, use_global_device_ids=true | all-gather | bytes 983040 | tf_op jit(solution)/shard_map/all_gather | solution.py:169
  98.8 17.9 %all-gather.1 = bf16[2048,192]{0,1:T(8,128)(2,1)S(1)} all-gather(bf16[512,192]{0,1:T(8,128)(2,1)S(1)} %fusion.71), channel_id=3, replica_groups=mesh['shard'=2,'context'=4,'tensor'=4] {'context'}, dimensions={0}, use_global_device_ids=true | all-gather | bytes 983040 | tf_op jit(solution)/shard_map/all_gather | solution.py:170
  116.7 19.4 %all-gather.3 = bf16[2048,192]{0,1:T(8,128)(2,1)S(1)} all-gather(bf16[512,192]{0,1:T(8,128)(2,1)S(1)} %fusion.73), channel_id=5, replica_groups=mesh['shard'=2,'context'=4,'tensor'=4] {'context'}, dimensions={0}, use_global_device_ids=true | all-gather | bytes 983040 | tf_op jit(solution)/shard_map/all_gather | solution.py:170
  136.1 15.8 %all-gather.5 = bf16[2048,192]{0,1:T(8,128)(2,1)S(1)} all-gather(bf16[512,192]{0,1:T(8,128)(2,1)S(1)} %fusion.75), channel_id=7, replica_groups=mesh['shard'=2,'context'=4,'tensor'=4] {'context'}, dimensions={0}, use_global_device_ids=true | all-gather | bytes 983040 | tf_op jit(solution)/shard_map/all_gather | solution.py:170
  174.4 93.1 %all-reduce.18.cloned.1.call-done = (f32[512,768]{1,0:T(8,128)}, f32[512,768]{1,0:T(8,128)}, f32[512,768]{1,0:T(8,128)}) async-done(((f32[512,768]{1,0:T(8,128)}, f32[512,768]{1,0:T(8,128)}, f32[512,768]{1,0:T(8,128)}), (f32[512,768]{1,0:T(8,128)}, f32[512,768]{1,0:T(8,128)}, f32[512,768]{1,0:T(8,128)})) %all-reduce.18.cloned.1.call-update) | async-done | bytes 4718608 | tf_op jit(solution)/shard_map/psum | solution.py:174
  272.5 6.9 multiply_convert_fusion.10
  299.2 94.5 %all-reduce.16.cloned.1.call-done = (f32[512,768]{1,0:T(8,128)}, f32[512,768]{1,0:T(8,128)}, f32[512,768]{1,0:T(8,128)}) async-done(((f32[512,768]{1,0:T(8,128)}, f32[512,768]{1,0:T(8,128)}, f32[512,768]{1,0:T(8,128)}), (f32[512,768]{1,0:T(8,128)}, f32[512,768]{1,0:T(8,128)}, f32[512,768]{1,0:T(8,128)})) %all-reduce.16.cloned.1.call-update) | async-done | bytes 4718608 | tf_op jit(solution)/shard_map/psum | solution.py:184
  421.8 94.4 %all-reduce.14.cloned.1.call-done = (f32[512,768]{1,0:T(8,128)}, f32[512,768]{1,0:T(8,128)}, f32[512,768]{1,0:T(8,128)}) async-done(((f32[512,768]{1,0:T(8,128)}, f32[512,768]{1,0:T(8,128)}, f32[512,768]{1,0:T(8,128)}), (f32[512,768]{1,0:T(8,128)}, f32[512,768]{1,0:T(8,128)}, f32[512,768]{1,0:T(8,128)})) %all-reduce.14.cloned.1.call-update) | async-done | bytes 4718608 | tf_op jit(solution)/shard_map/psum | solution.py:208
  679.6 34.8 %reduce-scatter.27.cloned.1.call-done = f32[1,512,192]{1,2,0:T(8,128)} async-done(((f32[1,2048,192]{1,2,0:T(8,128)}), f32[1,512,192]{1,2,0:T(8,128)}) %reduce-scatter.27.cloned.1.call-update) | async-done | bytes 393232 | tf_op jit(solution)/shard_map/reduce_scatter | solution.py:228
  716.8 34.0 %reduce-scatter.31.cloned.1.call-done = f32[1,512,192]{1,2,0:T(8,128)} async-done(((f32[1,2048,192]{1,2,0:T(8,128)}), f32[1,512,192]{1,2,0:T(8,128)}) %reduce-scatter.31.cloned.1.call-update) | async-done | bytes 393232 | tf_op jit(solution)/shard_map/reduce_scatter | solution.py:228
  760.4 13.6 %reduce-scatter.45.cloned.1.call-done = bf16[384,768]{1,0:T(8,128)(2,1)} async-done(((bf16[768,768]{1,0:T(8,128)(2,1)}), bf16[384,768]{1,0:T(8,128)(2,1)}) %reduce-scatter.45.cloned.1.call-update) | async-done | bytes 589840
  778.6 10.8 %reduce-scatter.43.cloned.1.call-done = bf16[384,192]{1,0:T(8,128)(2,1)} async-done(((bf16[768,192]{1,0:T(8,128)(2,1)}), bf16[384,192]{1,0:T(8,128)(2,1)}) %reduce-scatter.43.cloned.1.call-update) | async-done | bytes 147472
  791.2 14.0 %reduce-scatter.37.cloned.1.call-done = bf16[384,192]{1,0:T(8,128)(2,1)} async-done(((bf16[768,192]{1,0:T(8,128)(2,1)}), bf16[384,192]{1,0:T(8,128)(2,1)}) %reduce-scatter.37.cloned.1.call-update) | async-done | bytes 147472
  806.9 13.7 %reduce-scatter.41.cloned.1.call-done = bf16[384,192]{1,0:T(8,128)(2,1)} async-done(((bf16[768,192]{1,0:T(8,128)(2,1)}), bf16[384,192]{1,0:T(8,128)(2,1)}) %reduce-scatter.41.cloned.1.call-update) | async-done | bytes 147472
  822.3 13.4 %reduce-scatter.39.cloned.1.call-done = bf16[384,192]{1,0:T(8,128)(2,1)} async-done(((bf16[768,192]{1,0:T(8,128)(2,1)}), bf16[384,192]{1,0:T(8,128)(2,1)}) %reduce-scatter.39.cloned.1.call-update) | async-done | bytes 147472
  837.4 22.9 %reduce-scatter.35.cloned.1.call-done = bf16[384,768]{1,0:T(8,128)(2,1)} async-done(((bf16[768,768]{1,0:T(8,128)(2,1)}), bf16[384,768]{1,0:T(8,128)(2,1)}) %reduce-scatter.35.cloned.1.call-update) | async-done | bytes 589840 | tf_op jit(solution)/shard_map/reduce_scatter | solution.py:268
  874.0 38.7 %all-reduce = (f32[192]{0:T(256)}, f32[192]{0:T(256)}, f32[768]{0:T(1024)}, f32[768]{0:T(1024)}, f32[768]{0:T(1024)}, /*index=5*/f32[768]{0:T(1024)}, f32[768]{0:T(1024)}, f32[768]{0:T(1024)}, f32[768]{0:T(1024)}) all-reduce(f32[192]{0:T(256)S(1)} %add_add_fusion.17, ...), channel_id=1, replica_groups=mesh['shard'=2,'context'=4,'tensor'=4] {'shard','context'}, use_global_device_ids=true, to_apply=%region_74.0 | all-reduce | flops 5760 | bytes 46080 | tf_op jit(solution)/shard_map/psum | solution.py:283
  912.7 30.0 %all-reduce.20.cloned.1.call-done = (bf16[384,192]{0,1:T(8,128)(2,1)}, bf16[384,192]{0,1:T(8,128)(2,1)}, bf16[384,192]{0,1:T(8,128)(2,1)}, bf16[192,384]{1,0:T(8...) async-done(((bf16[384,192]{0,1:T(8,128)(2,1)}, bf16[384,192]{0,1:T(8,128)(2,1)}, bf16[384,192]{0,1:T(8,128)(2,1)}, bf16[192,384]{1,0:T(8,128)(2,1)}, ...) | async-done | bytes 1769488 | tf_op jit(solution)/shard_map/psum | solution.py:276
  949.3 89.8 %all-reduce.12.cloned.1.call-done = (f32[512,768]{1,0:T(8,128)}, f32[512,768]{1,0:T(8,128)}, f32[512,768]{1,0:T(8,128)}) async-done(((f32[512,768]{1,0:T(8,128)}, f32[512,768]{1,0:T(8,128)}, f32[512,768]{1,0:T(8,128)}), (f32[512,768]{1,0:T(8,128)}, f32[512,768]{1,0:T(8,128)}, f32[512,768]{1,0:T(8,128)})) %all-reduce.12.cloned.1.call-update) | async-done | bytes 4718608 | tf_op jit(solution)/shard_map/psum | solution.py:252
  (692 shorter events, 308.9 us)
Async XLA Ops:
  8.0 259.5 %all-reduce.18.cloned.1.call-start = ((), (), s32[]{:S(2)}) async-start(), calls=%async_computation.29 | async-start | bytes 9437184 | tf_op jit(solution)/shard_map/psum | solution.py:174
  153.6 397.4 %copy-start.165 = (f32[512]{0:T(512)}, f32[512]{0:T(512)S(1)}, u32[]{:S(2)}) copy-start(f32[512]{0:T(512)S(1)} %log_add_fusion.1) | copy-start | bytes 6148
  156.3 395.8 %copy-start.163 = (f32[512]{0:T(512)}, f32[512]{0:T(512)S(1)}, u32[]{:S(2)}) copy-start(f32[512]{0:T(512)S(1)} %log_add_fusion.2) | copy-start | bytes 6148
  173.2 99.3 %all-gather.9.cloned.1.call-start = ((), (), s32[]{:S(2)}) async-start(), calls=%async_computation.12 | async-start | bytes 1769472 | tf_op jit(solution)/shard_map/all_gather | solution.py:150
  173.8 111.3 %all-gather.11.cloned.1.call-start = ((), (), s32[]{:S(2)}) async-start(), calls=%async_computation.13 | async-start | bytes 1769472 | tf_op jit(solution)/shard_map/all_gather | solution.py:151
  174.4 219.3 %all-reduce.16.cloned.1.call-start = ((), (), s32[]{:S(2)}) async-start(), calls=%async_computation.28 | async-start | bytes 9437184 | tf_op jit(solution)/shard_map/psum | solution.py:184
  271.3 261.6 %copy-start.161 = (f32[512]{0:T(512)}, f32[512]{0:T(512)S(1)}, u32[]{:S(2)}) copy-start(f32[512]{0:T(512)S(1)} %broadcast_multiply_fusion.15) | copy-start | bytes 6148
  271.7 248.5 %copy-start.168 = (f32[512]{0:T(512)}, f32[512]{0:T(512)S(1)}, u32[]{:S(2)}) copy-start(f32[512]{0:T(512)S(1)} %add_rsqrt_fusion.5) | copy-start | bytes 6148
  272.5 260.5 %copy-start.170 = (f32[512]{0:T(512)}, f32[512]{0:T(512)S(1)}, u32[]{:S(2)}) copy-start(f32[512]{0:T(512)S(1)} %add_rsqrt_fusion.3) | copy-start | bytes 6148
  299.0 217.2 %all-reduce.14.cloned.1.call-start = ((), (), s32[]{:S(2)}) async-start(), calls=%async_computation.27 | async-start | bytes 9437184 | tf_op jit(solution)/shard_map/psum | solution.py:208
  421.5 246.6 %reduce-scatter.25.cloned.1.call-start = ((), (), s32[]{:S(2)}) async-start(), calls=%async_computation.15 | async-start | bytes 1966080 | tf_op jit(solution)/shard_map/reduce_scatter | solution.py:229
  532.8 136.9 %reduce-scatter.29.cloned.1.call-start = ((), (), s32[]{:S(2)}) async-start(), calls=%async_computation.17 | async-start | bytes 1966080 | tf_op jit(solution)/shard_map/reduce_scatter | solution.py:229
  545.4 126.0 %reduce-scatter.33.cloned.1.call-start = ((), (), s32[]{:S(2)}) async-start(), calls=%async_computation.19 | async-start | bytes 1966080 | tf_op jit(solution)/shard_map/reduce_scatter | solution.py:229
  565.1 112.9 %reduce-scatter.23.cloned.1.call-start = ((), (), s32[]{:S(2)}) async-start(), calls=%async_computation.14 | async-start | bytes 1966080 | tf_op jit(solution)/shard_map/reduce_scatter | solution.py:228
  591.7 122.7 %reduce-scatter.27.cloned.1.call-start = ((), (), s32[]{:S(2)}) async-start(), calls=%async_computation.16 | async-start | bytes 1966080 | tf_op jit(solution)/shard_map/reduce_scatter | solution.py:228
  615.0 135.8 %reduce-scatter.31.cloned.1.call-start = ((), (), s32[]{:S(2)}) async-start(), calls=%async_computation.18 | async-start | bytes 1966080 | tf_op jit(solution)/shard_map/reduce_scatter | solution.py:228
  629.9 144.1 %reduce-scatter.45.cloned.1.call-start = ((), (), s32[]{:S(2)}) async-start(), calls=%async_computation.25 | async-start | bytes 1769472
  642.2 147.2 %reduce-scatter.43.cloned.1.call-start = ((), (), s32[]{:S(2)}) async-start(), calls=%async_computation.24 | async-start | bytes 589824
  661.5 143.7 %reduce-scatter.37.cloned.1.call-start = ((), (), s32[]{:S(2)}) async-start(), calls=%async_computation.21 | async-start | bytes 589824
  668.0 152.5 %reduce-scatter.41.cloned.1.call-start = ((), (), s32[]{:S(2)}) async-start(), calls=%async_computation.23 | async-start | bytes 589824
  673.9 161.8 %reduce-scatter.39.cloned.1.call-start = ((), (), s32[]{:S(2)}) async-start(), calls=%async_computation.22 | async-start | bytes 589824
  753.5 106.8 %reduce-scatter.35.cloned.1.call-start = ((), (), s32[]{:S(2)}) async-start(), calls=%async_computation.20 | async-start | bytes 1769472 | tf_op jit(solution)/shard_map/reduce_scatter | solution.py:268
  758.1 184.6 %all-reduce.20.cloned.1.call-start = ((), (), s32[]{:S(2)}) async-start(), calls=%async_computation.30 | async-start | bytes 3538944 | tf_op jit(solution)/shard_map/psum | solution.py:276
  860.3 178.7 %all-reduce.12.cloned.1.call-start = ((), (), s32[]{:S(2)}) async-start(), calls=%async_computation.26 | async-start | bytes 9437184 | tf_op jit(solution)/shard_map/psum | solution.py:252
  (207 other events, 2294.0 us)
Sparse Core Ops, SparseCore 0:
  173.3 94.1 all-reduce.17
  299.1 94.5 all-reduce.15
  421.6 94.5 all-reduce.13
Sparse Core Ops, SparseCore 1:
  175.2 22.4 all-gather.8
  199.1 22.6 all-gather.10
  532.9 35.4 reduce-scatter.24
  570.7 34.1 reduce-scatter.28
  607.2 34.1 reduce-scatter.32
  643.8 34.2 reduce-scatter.22
  680.2 34.1 reduce-scatter.26
  716.5 34.1 reduce-scatter.30
  753.4 20.5 reduce-scatter.44
  776.4 13.0 reduce-scatter.42
  792.1 13.0 reduce-scatter.36
  807.5 13.0 reduce-scatter.40
  822.7 13.0 reduce-scatter.38
  838.6 21.6 reduce-scatter.34
  864.3 78.3 all-reduce.19
  946.0 93.0 all-reduce.11
where the time goes:
time: 1060 us
  waiting for transfers between devices  564 us (53%)
  blocking collectives  168 us (16%)
  matrix products  167 us (16%)
  other arithmetic  80.6 us (8%)
  local copies, waits for them, and re-layouts  54.3 us (5%)
  between operations  18.8 us (2%)
    psum x1, waiting for transfers between devices, on_device(): lax.psum(jnp.dot(activated_low, full_down, preferred_element_type=jnp.flo...  94.5 us
    psum x1, waiting for transfers between devices, on_device(): lax.psum(jnp.einsum('rf,df->rd', grad_inner, full_hidden, preferred_eleme...  94.4 us
    psum x1, waiting for transfers between devices, on_device(): lax.psum(jnp.dot(attended_rows, full_out, preferred_element_type=jnp.floa...  93.1 us
    psum x1, waiting for transfers between devices, on_device(): grad_input = grad_pre_first + lax.psum(back_rows, 'tensor')  89.8 us
    reduce_scatter x3, waiting for transfers between devices, on_device(): lax.psum_scatter(grad_keys, 'context', scatter_dimension=1, tiled=True)  72.8 us
    unnamed x24, waiting for transfers between devices  66.9 us
    unnamed x434, local copies, waits for them, and re-layouts  54.3 us
    all_gather x3, blocking collectives, on_device(): lax.all_gather(local_values, 'context', axis=1, tiled=True)  53.1 us
  transfers between devices with their start and end apart: 19, of which 14 were waited for; matrix products, arithmetic and copies ran while one was open for 16% of the time, Pallas kernels for 0%

commit v1 on v0

--- a/solution.py
+++ b/solution.py
@@ -6,6 +6,34 @@
 HEAD_DIM = 64
 MICRO = 3
 EPSILON = 1e-05
+
+
+def unite_links(vec, mesh_ax):
+    sheets = []
+    piece_out, tmp, state_next = (lax.axis_size(mesh_ax), lax.axis_index(mesh_ax), vec.shape[1])
+    for s, ix in enumerate(vec.shape):
+        sheets.append(ix * piece_out if s == 1 else ix)
+    latest = lax.dynamic_update_slice_in_dim(
+        jnp.zeros(sheets, vec.dtype), vec, tmp * state_next, axis=1
+    )
+    far_arr = side_arr = vec
+    for p in range(1, piece_out // 2 + 1):
+        rack = []
+        for s in range(piece_out):
+            rack.append((s, (s + 1) % piece_out))
+        far_arr = lax.ppermute(far_arr, axis_name=mesh_ax, perm=rack)
+        latest = lax.dynamic_update_slice_in_dim(
+            latest, far_arr, (tmp - p) % piece_out * state_next, axis=1
+        )
+        if 2 * p < piece_out:
+            rows = []
+            for s in range(piece_out):
+                rows.append((s, (s - 1) % piece_out))
+            side_arr = lax.ppermute(side_arr, mesh_ax, perm=rows)
+            latest = lax.dynamic_update_slice_in_dim(
+                latest, side_arr, (tmp + p) % piece_out * state_next, axis=1
+            )
+    return latest
 
 
 def layer_norm(values, gain, bias):
@@ -167,7 +195,7 @@
         local_values = value_low.reshape(per_micro, part_len, head_cols)
         all_keys, all_values = (
             lax.all_gather(local_keys, "context", axis=1, tiled=True),
-            lax.all_gather(local_values, "context", axis=1, tiled=True),
+            unite_links(local_values, "context"),
         )
         attended, totals = attend(queries, all_keys, all_values, factor)
         attended_rows = attended.reshape(row_count, head_cols)

time: 1060 us -> 948 us (0.89)
  waiting for transfers between devices: 564 us -> 476 us
  blocking collectives: 168 us -> 116 us
  local copies, waits for them, and re-layouts: 54.3 us -> 68 us
  starting transfers between devices: 2.54 us -> 14.4 us
    psum x1, waiting for transfers between devices: 89.8 us -> 0.01 us  [on_device(): grad_input = grad_pre_first + lax.psum(back_rows, 'tensor')]
    all_gather x3 -> x0, blocking collectives: 53.1 us -> none  [on_device(): lax.all_gather(local_values, 'context', axis=1, tiled=True)]
    ppermute x0 -> x9, starting transfers between devices: none -> 11.4 us  [the longest x3 7.91 us: unite_links(): side_arr = lax.ppermute(side_arr, mesh_ax, perm=rows)]
    unnamed x24, waiting for transfers between devices: 66.9 us -> 55.5 us
    unnamed x434 -> x448, local copies, waits for them, and re-layouts: 54.3 us -> 64.8 us
  transfers between devices with their start and end apart: 19 -> 28, of which waited for: 14 -> 14; matrix products, arithmetic and copies ran while one was open for 16% -> 21% of each run, Pallas kernels for 0% -> 0%
where the time goes in v1:
time: 948 us; the launch traced here: 940 us
  waiting for transfers between devices  476 us (50%)
  matrix products  168 us (18%)
  blocking collectives  116 us (12%)
  other arithmetic  79.2 us (8%)
  local copies, waits for them, and re-layouts  68 us (7%)
  between operations  18.9 us (2%)
  starting transfers between devices  14.4 us (2%)
    psum x1, waiting for transfers between devices, on_device(): lax.psum(jnp.dot(activated_low, full_down, preferred_element_type=jnp.flo...  94.5 us
    psum x1, waiting for transfers between devices, on_device(): lax.psum(jnp.einsum('rf,df->rd', grad_inner, full_hidden, preferred_eleme...  94.4 us
    psum x1, waiting for transfers between devices, on_device(): lax.psum(jnp.dot(attended_rows, full_out, preferred_element_type=jnp.floa...  92.3 us
    reduce_scatter x3, waiting for transfers between devices, on_device(): lax.psum_scatter(grad_keys, 'context', scatter_dimension=1, tiled=True)  72.4 us
    unnamed x448, local copies, waits for them, and re-layouts  64.8 us
    unnamed x24, waiting for transfers between devices  55.5 us
    all_gather x3, blocking collectives, on_device(): lax.all_gather(local_keys, 'context', axis=1, tiled=True)  51.8 us
    psum x1, waiting for transfers between devices, on_device(): lax.psum(owned[0].astype(jnp.bfloat16), 'context').astype(jnp.float32)  38.7 us
  transfers between devices with their start and end apart: 28, of which 14 were waited for; matrix products, arithmetic and copies ran while one was open for 21% of the time, Pallas kernels for 0%

profile of v1, /device:TPU:0, one launch (start us, length us, event | category | flops | bytes accessed | tf_op | source)
XLA Modules:
  0.0 939.8 jit_solution(10561275189795145511)
XLA Ops:
  8.1 7.7 all_gather.42
  28.4 5.8 all_gather.18
  35.6 5.8 all_gather.19
  42.6 18.0 %all-gather.2 = bf16[2048,192]{0,1:T(8,128)(2,1)S(1)} all-gather(bf16[512,192]{0,1:T(8,128)(2,1)S(1)} %convolution_convert_fusion.3), channel_id=4, replica_groups=mesh['shard'=2,'context'=4,'tensor'=4] {'context'}, dimensions={0}, use_global_device_ids=true | all-gather | bytes 983040 | tf_op jit(solution)/shard_map/all_gather | solution.py:197
  63.1 17.9 %all-gather.1 = bf16[2048,192]{0,1:T(8,128)(2,1)S(1)} all-gather(bf16[512,192]{0,1:T(8,128)(2,1)S(1)} %convolution_convert_fusion.4), channel_id=3, replica_groups=mesh['shard'=2,'context'=4,'tensor'=4] {'context'}, dimensions={0}, use_global_device_ids=true | all-gather | bytes 983040 | tf_op jit(solution)/shard_map/all_gather | solution.py:197
  83.5 15.9 %all-gather = bf16[2048,192]{0,1:T(8,128)(2,1)S(1)} all-gather(bf16[512,192]{0,1:T(8,128)(2,1)S(1)} %convolution_convert_fusion.5), channel_id=2, replica_groups=mesh['shard'=2,'context'=4,'tensor'=4] {'context'}, dimensions={0}, use_global_device_ids=true | all-gather | bytes 983040 | tf_op jit(solution)/shard_map/all_gather | solution.py:197
  109.6 5.8 all_gather.43
  154.4 92.3 %all-reduce.18.cloned.1.call-done = (f32[512,768]{1,0:T(8,128)}, f32[512,768]{1,0:T(8,128)}, f32[512,768]{1,0:T(8,128)}) async-done(((f32[512,768]{1,0:T(8,128)}, f32[512,768]{1,0:T(8,128)}, f32[512,768]{1,0:T(8,128)}), (f32[512,768]{1,0:T(8,128)}, f32[512,768]{1,0:T(8,128)}, f32[512,768]{1,0:T(8,128)})) %all-reduce.18.cloned.1.call-update) | async-done | bytes 4718608 | tf_op jit(solution)/shard_map/psum | solution.py:202
  251.7 6.9 multiply_convert_fusion.10
  258.5 5.6 multiply_convert_fusion.9
  269.7 5.4 multiply_convert_fusion.11
  278.3 94.5 %all-reduce.16.cloned.1.call-done = (f32[512,768]{1,0:T(8,128)}, f32[512,768]{1,0:T(8,128)}, f32[512,768]{1,0:T(8,128)}) async-done(((f32[512,768]{1,0:T(8,128)}, f32[512,768]{1,0:T(8,128)}, f32[512,768]{1,0:T(8,128)}), (f32[512,768]{1,0:T(8,128)}, f32[512,768]{1,0:T(8,128)}, f32[512,768]{1,0:T(8,128)})) %all-reduce.16.cloned.1.call-update) | async-done | bytes 4718608 | tf_op jit(solution)/shard_map/psum | solution.py:212
  400.9 94.4 %all-reduce.14.cloned.1.call-done = (f32[512,768]{1,0:T(8,128)}, f32[512,768]{1,0:T(8,128)}, f32[512,768]{1,0:T(8,128)}) async-done(((f32[512,768]{1,0:T(8,128)}, f32[512,768]{1,0:T(8,128)}, f32[512,768]{1,0:T(8,128)}), (f32[512,768]{1,0:T(8,128)}, f32[512,768]{1,0:T(8,128)}, f32[512,768]{1,0:T(8,128)})) %all-reduce.14.cloned.1.call-update) | async-done | bytes 4718608 | tf_op jit(solution)/shard_map/psum | solution.py:236
  534.9 5.3 multiply_reduce_fusion.6
  561.6 5.3 multiply_reduce_fusion.3
  658.7 34.8 %reduce-scatter.27.cloned.1.call-done = f32[1,512,192]{1,2,0:T(8,128)} async-done(((f32[1,2048,192]{1,2,0:T(8,128)}), f32[1,512,192]{1,2,0:T(8,128)}) %reduce-scatter.27.cloned.1.call-update) | async-done | bytes 393232 | tf_op jit(solution)/shard_map/reduce_scatter | solution.py:256
  695.9 34.0 %reduce-scatter.31.cloned.1.call-done = f32[1,512,192]{1,2,0:T(8,128)} async-done(((f32[1,2048,192]{1,2,0:T(8,128)}), f32[1,512,192]{1,2,0:T(8,128)}) %reduce-scatter.31.cloned.1.call-update) | async-done | bytes 393232 | tf_op jit(solution)/shard_map/reduce_scatter | solution.py:256
  755.8 12.7 %reduce-scatter.43.cloned.1.call-done = bf16[384,192]{1,0:T(8,128)(2,1)} async-done(((bf16[768,192]{1,0:T(8,128)(2,1)}), bf16[384,192]{1,0:T(8,128)(2,1)}) %reduce-scatter.43.cloned.1.call-update) | async-done | bytes 147472
  770.3 13.5 %reduce-scatter.37.cloned.1.call-done = bf16[384,192]{1,0:T(8,128)(2,1)} async-done(((bf16[768,192]{1,0:T(8,128)(2,1)}), bf16[384,192]{1,0:T(8,128)(2,1)}) %reduce-scatter.37.cloned.1.call-update) | async-done | bytes 147472
  785.5 13.7 %reduce-scatter.41.cloned.1.call-done = bf16[384,192]{1,0:T(8,128)(2,1)} async-done(((bf16[768,192]{1,0:T(8,128)(2,1)}), bf16[384,192]{1,0:T(8,128)(2,1)}) %reduce-scatter.41.cloned.1.call-update) | async-done | bytes 147472
  801.0 13.5 %reduce-scatter.39.cloned.1.call-done = bf16[384,192]{1,0:T(8,128)(2,1)} async-done(((bf16[768,192]{1,0:T(8,128)(2,1)}), bf16[384,192]{1,0:T(8,128)(2,1)}) %reduce-scatter.39.cloned.1.call-update) | async-done | bytes 147472
  816.1 22.9 %reduce-scatter.35.cloned.1.call-done = bf16[384,768]{1,0:T(8,128)(2,1)} async-done(((bf16[768,768]{1,0:T(8,128)(2,1)}), bf16[384,768]{1,0:T(8,128)(2,1)}) %reduce-scatter.35.cloned.1.call-update) | async-done | bytes 589840 | tf_op jit(solution)/shard_map/reduce_scatter | solution.py:296
  839.5 38.7 %all-reduce = (f32[192]{0:T(256)}, f32[192]{0:T(256)}, f32[768]{0:T(1024)}, f32[768]{0:T(1024)}, f32[768]{0:T(1024)}, /*index=5*/f32[768]{0:T(1024)}, f32[768]{0:T(1024)}, f32[768]{0:T(1024)}, f32[768]{0:T(1024)}) all-reduce(f32[192]{0:T(256)S(1)} %add_add_fusion.17, ...), channel_id=1, replica_groups=mesh['shard'=2,'context'=4,'tensor'=4] {'shard','context'}, use_global_device_ids=true, to_apply=%region_74.75 | all-reduce | flops 5760 | bytes 46080 | tf_op jit(solution)/shard_map/psum | solution.py:311
  884.4 38.7 %all-reduce.20.cloned.1.call-done = (bf16[384,192]{0,1:T(8,128)(2,1)}, bf16[384,192]{0,1:T(8,128)(2,1)}, bf16[384,192]{0,1:T(8,128)(2,1)}, bf16[192,384]{1,0:T(8...) async-done(((bf16[384,192]{0,1:T(8,128)(2,1)}, bf16[384,192]{0,1:T(8,128)(2,1)}, bf16[384,192]{0,1:T(8,128)(2,1)}, bf16[192,384]{1,0:T(8,128)(2,1)}, ...) | async-done | bytes 1769488 | tf_op jit(solution)/shard_map/psum | solution.py:304
  (733 shorter events, 311.7 us)
Async XLA Ops:
  8.0 238.6 %all-reduce.18.cloned.1.call-start = ((), (), s32[]{:S(2)}) async-start(), calls=%async_computation.29 | async-start | bytes 9437184 | tf_op jit(solution)/shard_map/psum | solution.py:202
  18.3 97.2 %collective-permute-start.3 = (bf16[1,512,192]{1,2,0:T(8,128)(2,1)}, bf16[1,512,192]{1,2,0:T(8,128)(2,1)S(1)}, u32[]{:S(2)}, u32[]{:S(2)}) collective-permute-start(bf16[1,512,192]{1,2,0:T(8,128)(2,1)} %get-tuple-element.139), channel_id=1, source_target_pairs={{0,4},{4,8},{8,12},{12,0},{1,5},{5,9},{9,13},{13,1},{2,6},{6,10},{... | collective-permute-start | bytes 589832 | tf_op jit(solution)/shard_map/ppermute | solution.py:24
  20.1 98.6 %collective-permute-start.4 = (bf16[1,512,192]{1,2,0:T(8,128)(2,1)}, bf16[1,512,192]{1,2,0:T(8,128)(2,1)}, u32[]{:S(2)}, u32[]{:S(2)}) collective-permute-start(bf16[1,512,192]{1,2,0:T(8,128)(2,1)} %get-tuple-element.139), channel_id=1, source_target_pairs={{0,12},{4,0},{8,4},{12,8},{1,13},{5,1},{9,5},{13,9},{2,14},{6,2},{... | collective-permute-start | bytes 589832 | tf_op jit(solution)/shard_map/ppermute | solution.py:32
  23.3 94.2 %collective-permute-start.6 = (bf16[1,512,192]{1,2,0:T(8,128)(2,1)}, bf16[1,512,192]{1,2,0:T(8,128)(2,1)}, u32[]{:S(2)}, u32[]{:S(2)}) collective-permute-start(bf16[1,512,192]{1,2,0:T(8,128)(2,1)} %get-tuple-element.131), channel_id=1, source_target_pairs={{0,4},{4,8},{8,12},{12,0},{1,5},{5,9},{9,13},{13,1},{2,6},{6,10},{... | collective-permute-start | bytes 589832 | tf_op jit(solution)/shard_map/ppermute | solution.py:24
  23.3 97.9 %collective-permute-start.7 = (bf16[1,512,192]{1,2,0:T(8,128)(2,1)}, bf16[1,512,192]{1,2,0:T(8,128)(2,1)}, u32[]{:S(2)}, u32[]{:S(2)}) collective-permute-start(bf16[1,512,192]{1,2,0:T(8,128)(2,1)} %get-tuple-element.131), channel_id=1, source_target_pairs={{0,12},{4,0},{8,4},{12,8},{1,13},{5,1},{9,5},{13,9},{2,14},{6,2},{... | collective-permute-start | bytes 589832 | tf_op jit(solution)/shard_map/ppermute | solution.py:32
  28.4 90.2 %collective-permute-start = (bf16[1,512,192]{1,2,0:T(8,128)(2,1)}, bf16[1,512,192]{1,2,0:T(8,128)(2,1)S(1)}, u32[]{:S(2)}, u32[]{:S(2)}) collective-permute-start(bf16[1,512,192]{1,2,0:T(8,128)(2,1)} %get-tuple-element.147), channel_id=1, source_target_pairs={{0,4},{4,8},{8,12},{12,0},{1,5},{5,9},{9,13},{13,1},{2,6},{6,10},{... | collective-permute-start | bytes 589832 | tf_op jit(solution)/shard_map/ppermute | solution.py:24
  152.7 98.9 %all-gather.6.cloned.1.call-start = ((), (), s32[]{:S(2)}) async-start(), calls=%async_computation.12 | async-start | bytes 1769472 | tf_op jit(solution)/shard_map/all_gather | solution.py:178
  153.3 110.9 %all-gather.8.cloned.1.call-start = ((), (), s32[]{:S(2)}) async-start(), calls=%async_computation.13 | async-start | bytes 1769472 | tf_op jit(solution)/shard_map/all_gather | solution.py:179
  153.9 218.9 %all-reduce.16.cloned.1.call-start = ((), (), s32[]{:S(2)}) async-start(), calls=%async_computation.28 | async-start | bytes 9437184 | tf_op jit(solution)/shard_map/psum | solution.py:212
  278.1 217.3 %all-reduce.14.cloned.1.call-start = ((), (), s32[]{:S(2)}) async-start(), calls=%async_computation.27 | async-start | bytes 9437184 | tf_op jit(solution)/shard_map/psum | solution.py:236
  400.6 247.0 %reduce-scatter.25.cloned.1.call-start = ((), (), s32[]{:S(2)}) async-start(), calls=%async_computation.15 | async-start | bytes 1966080 | tf_op jit(solution)/shard_map/reduce_scatter | solution.py:257
  512.0 137.3 %reduce-scatter.29.cloned.1.call-start = ((), (), s32[]{:S(2)}) async-start(), calls=%async_computation.17 | async-start | bytes 1966080 | tf_op jit(solution)/shard_map/reduce_scatter | solution.py:257
  524.6 126.3 %reduce-scatter.33.cloned.1.call-start = ((), (), s32[]{:S(2)}) async-start(), calls=%async_computation.19 | async-start | bytes 1966080 | tf_op jit(solution)/shard_map/reduce_scatter | solution.py:257
  544.3 112.8 %reduce-scatter.23.cloned.1.call-start = ((), (), s32[]{:S(2)}) async-start(), calls=%async_computation.14 | async-start | bytes 1966080 | tf_op jit(solution)/shard_map/reduce_scatter | solution.py:256
  571.1 122.4 %reduce-scatter.27.cloned.1.call-start = ((), (), s32[]{:S(2)}) async-start(), calls=%async_computation.16 | async-start | bytes 1966080 | tf_op jit(solution)/shard_map/reduce_scatter | solution.py:256
  594.4 135.5 %reduce-scatter.31.cloned.1.call-start = ((), (), s32[]{:S(2)}) async-start(), calls=%async_computation.18 | async-start | bytes 1966080 | tf_op jit(solution)/shard_map/reduce_scatter | solution.py:256
  609.3 143.8 %reduce-scatter.45.cloned.1.call-start = ((), (), s32[]{:S(2)}) async-start(), calls=%async_computation.25 | async-start | bytes 1769472
  621.7 146.9 %reduce-scatter.43.cloned.1.call-start = ((), (), s32[]{:S(2)}) async-start(), calls=%async_computation.24 | async-start | bytes 589824
  641.0 142.8 %reduce-scatter.37.cloned.1.call-start = ((), (), s32[]{:S(2)}) async-start(), calls=%async_computation.21 | async-start | bytes 589824
  647.6 151.7 %reduce-scatter.41.cloned.1.call-start = ((), (), s32[]{:S(2)}) async-start(), calls=%async_computation.23 | async-start | bytes 589824
  653.4 161.0 %reduce-scatter.39.cloned.1.call-start = ((), (), s32[]{:S(2)}) async-start(), calls=%async_computation.22 | async-start | bytes 589824
  732.6 106.5 %reduce-scatter.35.cloned.1.call-start = ((), (), s32[]{:S(2)}) async-start(), calls=%async_computation.20 | async-start | bytes 1769472 | tf_op jit(solution)/shard_map/reduce_scatter | solution.py:296
  737.2 141.0 %all-reduce.12.cloned.1.call-start = ((), (), s32[]{:S(2)}) async-start(), calls=%async_computation.26 | async-start | bytes 9437184 | tf_op jit(solution)/shard_map/psum | solution.py:280
  747.1 176.0 %all-reduce.20.cloned.1.call-start = ((), (), s32[]{:S(2)}) async-start(), calls=%async_computation.30 | async-start | bytes 3538944 | tf_op jit(solution)/shard_map/psum | solution.py:304
  (223 other events, 3122.5 us)
Sparse Core Ops, SparseCore 0:
  152.8 93.7 all-reduce.17
  278.2 94.5 all-reduce.15
  400.8 94.5 all-reduce.13
  747.2 93.3 all-reduce.11
  844.4 78.6 all-reduce.19
Sparse Core Ops, SparseCore 1:
  154.7 22.0 all-gather.5
  178.2 22.6 all-gather.7
  512.0 35.4 reduce-scatter.24
  549.8 34.2 reduce-scatter.28
  586.4 34.1 reduce-scatter.32
  622.9 34.1 reduce-scatter.22
  659.3 34.1 reduce-scatter.26
  695.7 34.1 reduce-scatter.30
  732.6 20.5 reduce-scatter.44
  755.5 13.0 reduce-scatter.42
  770.7 13.0 reduce-scatter.36
  786.2 13.0 reduce-scatter.40
  801.3 13.0 reduce-scatter.38
  817.4 21.7 reduce-scatter.34
